TPU v7x, 32 devices: a whole 2x2x4 slice. The times are simulated.
32 devices in a mesh: row: 8 (over z, x), ch: 4 (over y, core).
Axes of the slice: x: 2, y: 2, z: 4, core: 2. Of those that a mesh axis runs over, the one named last changes fastest.
Arguments:
- pair_rep: bfloat16 [128, 8, 8], P('ch', 'row'), may hold values from -6 to 6
- residue_mask: int32 [8], replicated, may hold values 0 or 1
- chain_ids: int32 [8], replicated, may hold values from 0 to 3, never falling along the last dimension, each value on 1 to 4 neighbouring positions
- in_gain: float32 [2, 128], replicated, may hold values from 0.5 to 1.5
- in_bias: float32 [2, 128], replicated, may hold values from -3 to 3
- w_proj: bfloat16 [2, 128, 4, 128], P(None, None, None, 'ch'), may hold values from -0.5 to 0.5
- w_gate: bfloat16 [2, 128, 128], P(None, None, 'ch'), may hold values from -0.5 to 0.5
- pair_bias: float32 [2, 128], P(None, 'ch'), may hold values from -4 to 4
- out_gain: float32 [2, 128], P(None, 'ch'), may hold values from 0.5 to 1.5
- out_bias: float32 [2, 128], P(None, 'ch'), may hold values from -3 to 3
- w_out: bfloat16 [2, 128, 128], P(None, 'ch'), may hold values from -0.5 to 0.5
Outputs:
- pair_out: bfloat16 [128, 8, 8], P('ch', 'row')
Inputs may be any that keep to these rules, and one draw needn't show every extreme that they name: `chain_ids`: chain numbers never fall along the residues; each chain has 1 to 4 residues.
All inputs are finite; a program needn't handle non-finite values.
Results may differ from a plain program's by a relative error of at most 0.013.
Values may be sent and summed in bfloat16 or wider, within the bound.
A program may use at most 64 MiB of HBM per device.

v0:
```python
import jax
import jax.numpy as jnp
from jax import lax
from jax.sharding import PartitionSpec as P

epsilon = 1e-05


def channel_norm(values, norm_gain, norm_bias):
    mean_val = jnp.mean(values, axis=0)
    variance = jnp.mean(values * values, axis=0) - mean_val * mean_val
    return (values - mean_val) * lax.rsqrt(variance + epsilon) * norm_gain[
        :, None, None
    ] + norm_bias[:, None, None]


def prepare(
    pair_local, layer, in_gain, in_bias, w_proj, w_gate, pair_bias, mask_rows, mask_cols, same_chain
):
    full_pair = lax.all_gather(pair_local, "ch", axis=0, tiled=True)
    normed = channel_norm(full_pair.astype(jnp.float32), in_gain[layer], in_bias[layer]).astype(
        jnp.bfloat16
    )
    projected = jnp.einsum(
        "cij,cpd->pdij", normed, w_proj[layer], preferred_element_type=jnp.float32
    )
    pair_mask = mask_rows[:, None] * mask_cols[None, :]
    first_arm = (jax.nn.sigmoid(projected[0]) * projected[1] * pair_mask).astype(jnp.bfloat16)
    second_arm = (jax.nn.sigmoid(projected[2]) * projected[3] * pair_mask).astype(jnp.bfloat16)
    logits = jnp.einsum("cij,cd->dij", normed, w_gate[layer], preferred_element_type=jnp.float32)
    logits = logits + pair_bias[layer][:, None, None] * same_chain[None]
    return (first_arm, second_arm, jax.nn.sigmoid(logits))


def finish(product_sum, gating, layer, out_gain, out_bias, w_out):
    totals = lax.psum(
        (jnp.sum(product_sum, axis=0), jnp.sum(product_sum * product_sum, axis=0)), "ch"
    )
    channels = product_sum.shape[0] * lax.axis_size("ch")
    mean_val = totals[0] / channels
    variance = totals[1] / channels - mean_val * mean_val
    scaled = (product_sum - mean_val) * lax.rsqrt(variance + epsilon)
    normed = (scaled * out_gain[layer][:, None, None] + out_bias[layer][:, None, None]).astype(
        jnp.bfloat16
    )
    columns = w_out[layer]
    mixed = lax.psum_scatter(
        jnp.einsum("dij,dc->cij", normed, columns, preferred_element_type=jnp.float32).astype(
            jnp.bfloat16
        ),
        "ch",
        scatter_dimension=0,
        tiled=True,
    ).astype(jnp.float32)
    return gating * mixed


def body(
    pair_rep,
    residue_mask,
    chain_ids,
    in_gain,
    in_bias,
    w_proj,
    w_gate,
    pair_bias,
    out_gain,
    out_bias,
    w_out,
):
    rows_here = pair_rep.shape[1]
    row_start = lax.axis_index("row") * rows_here
    mask_cols = residue_mask.astype(jnp.float32)
    mask_rows = lax.dynamic_slice_in_dim(mask_cols, row_start, rows_here)
    chain_rows = lax.dynamic_slice_in_dim(chain_ids, row_start, rows_here)
    same_chain = (chain_rows[:, None] == chain_ids[None, :]).astype(jnp.float32)
    first_arm, second_arm, gating = prepare(
        pair_rep, 0, in_gain, in_bias, w_proj, w_gate, pair_bias, mask_rows, mask_cols, same_chain
    )
    product_sum = jnp.einsum(
        "cik,cjk->cij",
        first_arm,
        lax.all_gather(second_arm, "row", axis=1, tiled=True),
        preferred_element_type=jnp.float32,
    )
    middle = (
        pair_rep.astype(jnp.float32) + finish(product_sum, gating, 0, out_gain, out_bias, w_out)
    ).astype(jnp.bfloat16)
    in_first, in_second, in_gating = prepare(
        middle, 1, in_gain, in_bias, w_proj, w_gate, pair_bias, mask_rows, mask_cols, same_chain
    )
    exchanged_left = lax.all_to_all(in_first, "row", split_axis=2, concat_axis=1, tiled=True)
    left_rows = jnp.swapaxes(exchanged_left, 1, 2)
    in_product = jnp.einsum(
        "cik,ckj->cij",
        left_rows,
        lax.all_gather(in_second, "row", axis=1, tiled=True),
        preferred_element_type=jnp.float32,
    )
    update = finish(in_product, in_gating, 1, out_gain, out_bias, w_out)
    return (middle.astype(jnp.float32) + update).astype(jnp.bfloat16)


def solution(mesh):
    return jax.shard_map(
        body,
        mesh=mesh,
        in_specs=(
            P("ch", "row", None),
            P(),
            P(),
            P(),
            P(),
            P(None, None, None, "ch"),
            P(None, None, "ch"),
            P(None, "ch"),
            P(None, "ch"),
            P(None, "ch"),
            P(None, "ch", None),
        ),
        out_specs=P("ch", "row", None),
        check_vma=False,
    )
```

profile of v0, /device:TPU:0, one launch (start us, length us, event | category | flops | bytes accessed | tf_op | source)
XLA Modules:
  0.0 143.6 jit_solution(11897451887013223469)
XLA Ops:
  6.5 0.8 copy.22
  7.3 6.2 %all_gather.12 = bf16[128,1,8]{2,1,0:T(2,128)(2,1)S(1)} all-gather(bf16[32,1,8]{2,1,0:T(2,128)(2,1)S(1)} %copy.22), channel_id=1, replica_groups=mesh['row'=8,'ch'=4] {'ch'}, dimensions={0}, use_global_device_ids=true | all-gather | bytes 2560 | tf_op jit(solution)/shard_map/all_gather | solution.py:20
  13.6 0.2 convert_reduce_fusion.1
  13.8 0.6 copy-done.9
  14.4 0.6 dynamic_slice.7
  15.0 0.6 broadcast_multiply_fusion
  15.7 0.6 copy-done.2
  16.4 0.2 convolution_bitcast_fusion.1
  16.7 27.0 %all_gather.13 = bf16[32,8,8]{0,2,1:T(8,128)(2,1)S(1)} all-gather(bf16[32,1,8]{0,2,1:T(8,128)(2,1)S(1)} %fusion.56), channel_id=1, replica_groups=mesh['row'=8,'ch'=4] {'row'}, dimensions={1}, use_global_device_ids=true | all-gather | bytes 4608 | tf_op jit(solution)/shard_map/all_gather | solution.py:83
  43.8 5.7 %all-reduce.1 = (f32[1,8]{1,0:T(1,128)S(1)}, f32[1,8]{1,0:T(1,128)S(1)}) all-reduce(f32[1,8]{1,0:T(1,128)S(1)} %bitcast.174, f32[1,8]{1,0:T(1,128)S(1)} %bitcast.173), channel_id=1, replica_groups=mesh['row'=8,'ch'=4] {'ch'}, use_global_device_ids=true, to_apply=%region_5.0 | all-reduce | flops 16 | bytes 128 | tf_op jit(solution)/shard_map/psum | solution.py:36
  49.5 0.7 copy-done.4
  50.2 0.2 fusion.18
  50.4 0.7 copy.40
  51.1 0.6 copy-done.10
  51.7 0.6 dynamic_slice.6
  52.4 0.6 compare_convert_fusion
  53.1 17.3 %reduce-scatter.7.cloned.1.call-done = bf16[32,8]{1,0:T(8,128)(2,1)} async-done(((bf16[128,8]{1,0:T(8,128)(2,1)}), bf16[32,8]{1,0:T(8,128)(2,1)}) %reduce-scatter.7.cloned.1.call-update) | async-done | bytes 528
  70.4 0.8 copy.41
  71.2 0.2 fusion.17
  71.5 5.2 %all_gather.14 = bf16[128,1,8]{2,1,0:T(2,128)(2,1)S(1)} all-gather(bf16[32,1,8]{2,1,0:T(2,128)(2,1)S(1)} %copy.24), channel_id=1, replica_groups=mesh['row'=8,'ch'=4] {'ch'}, dimensions={0}, use_global_device_ids=true | all-gather | bytes 2560 | tf_op jit(solution)/shard_map/all_gather | solution.py:20
  76.8 0.2 convert_reduce_fusion
  77.0 0.2 convolution_bitcast_fusion
  77.2 0.6 copy.26
  77.9 5.5 %all-to-all-start = ((bf16[32,1,8]{0,1,2:T(2,128)(2,1)}), bf16[32,1,8]{0,1,2:T(2,128)(2,1)S(1)}, u32[]{:S(2)}, u32[]{:S(2)}) async-start(bf16[32,1,8]{0,1,2:T(2,128)(2,1)} %copy.26), calls=%async_computation | async-start | bytes 8192 | tf_op jit(solution)/shard_map/all_to_all | solution.py:92
  83.4 26.6 %all_gather.15 = bf16[32,8,8]{0,2,1:T(8,128)(2,1)S(1)} all-gather(bf16[32,1,8]{0,2,1:T(8,128)(2,1)S(1)} %get-tuple-element.18), channel_id=1, replica_groups=mesh['row'=8,'ch'=4] {'row'}, dimensions={1}, use_global_device_ids=true | all-gather | bytes 4608 | tf_op jit(solution)/shard_map/all_gather | solution.py:97
  110.1 0.1 fusion.83
  110.2 5.9 %all-reduce = (f32[1,8]{1,0:T(1,128)S(1)}, f32[1,8]{1,0:T(1,128)S(1)}) all-reduce(f32[1,8]{1,0:T(1,128)S(1)} %bitcast.176, f32[1,8]{1,0:T(1,128)S(1)} %bitcast.175), channel_id=1, replica_groups=mesh['row'=8,'ch'=4] {'ch'}, use_global_device_ids=true, to_apply=%region_12.0 | all-reduce | flops 16 | bytes 128 | tf_op jit(solution)/shard_map/psum | solution.py:36
  116.2 0.2 fusion.19
  116.4 0.7 copy.42
  117.1 18.1 %reduce-scatter.9.cloned.1.call-done = bf16[32,8]{1,0:T(8,128)(2,1)} async-done(((bf16[128,8]{1,0:T(8,128)(2,1)}), bf16[32,8]{1,0:T(8,128)(2,1)}) %reduce-scatter.9.cloned.1.call-update) | async-done | bytes 528
  135.2 0.8 copy.43
  136.0 0.8 fusion.16
  (41 shorter events, 0.9 us)
Async XLA Ops:
  6.5 63.9 %reduce-scatter.7.cloned.1.call-start = ((), (), s32[]{:S(2)}) async-start(), calls=%async_computation.3 | async-start | bytes 40960
  13.5 2.8 %copy-start.6 = (bf16[2,128,4,32]{1,3,2,0:T(8,128)(2,1)S(1)}, bf16[2,128,4,32]{1,3,2,0:T(8,128)(2,1)}, u32[]{:S(2)}) copy-start(bf16[2,128,4,32]{1,3,2,0:T(8,128)(2,1)} %param.16) | copy-start | bytes 196612
  13.8 0.7 copy-start.9
  15.7 0.7 copy-start.2
  15.7 0.7 copy-start.3
  43.7 6.5 %copy-start.7 = (bf16[2,32,128]{2,1,0:T(8,128)(2,1)S(1)}, bf16[2,32,128]{2,1,0:T(8,128)(2,1)}, u32[]{:S(2)}) copy-start(bf16[2,32,128]{2,1,0:T(8,128)(2,1)} %param.21) | copy-start | bytes 49156
  49.5 0.7 copy-start.4
  49.5 0.7 copy-start.5
  51.1 0.7 copy-start.10
  51.7 0.7 copy-start.1
  51.7 19.4 %copy-start.8 = (bf16[2,128,32]{1,2,0:T(8,128)(2,1)S(1)}, bf16[2,128,32]{1,2,0:T(8,128)(2,1)}, u32[]{:S(2)}) copy-start(bf16[2,128,32]{1,2,0:T(8,128)(2,1)} %param.17) | copy-start | bytes 49156
  53.1 18.1 %copy-start = (bf16[32,1,8]{0,2,1:T(8,128)(2,1)S(1)}, bf16[32,1,8]{0,2,1:T(8,128)(2,1)}, u32[]{:S(2)}) copy-start(bf16[32,1,8]{0,2,1:T(8,128)(2,1)} %param.11) | copy-start | bytes 1540
  77.9 32.2 %all-to-all-start = ((bf16[32,1,8]{0,1,2:T(2,128)(2,1)}), bf16[32,1,8]{0,1,2:T(2,128)(2,1)S(1)}, u32[]{:S(2)}, u32[]{:S(2)}) async-start(bf16[32,1,8]{0,1,2:T(2,128)(2,1)} %copy.26), calls=%async_computation | async-start | bytes 8192 | tf_op jit(solution)/shard_map/all_to_all | solution.py:92
  83.4 51.9 %reduce-scatter.9.cloned.1.call-start = ((), (), s32[]{:S(2)}) async-start(), calls=%async_computation.4 | async-start | bytes 40960
Sparse Core Ops, SparseCore 0:
  51.2 19.1 reduce-scatter.6
  117.2 17.9 reduce-scatter.8
where the time goes:
time: 144 us
  blocking collectives  76.7 us (53%)
  waiting for transfers between devices  35.5 us (25%)
  between operations  13.5 us (9%)
  local copies, waits for them, and re-layouts  8.5 us (6%)
  starting transfers between devices  5.55 us (4%)
  other arithmetic  2.19 us (2%)
  matrix products  1.71 us (1%)
    unnamed x4, waiting for transfers between devices  35.5 us
    all_gather x1, blocking collectives, body(): lax.all_gather(second_arm, 'row', axis=1, tiled=True)  27 us
    all_gather x1, blocking collectives, body(): lax.all_gather(in_second, 'row', axis=1, tiled=True)  26.6 us
    psum x2, blocking collectives, finish(): lax.psum((jnp.sum(product_sum, axis=0), jnp.sum(product_sum * product_sum...  11.6 us
    all_gather x2, blocking collectives, prepare(): full_pair = lax.all_gather(pair_local, 'ch', axis=0, tiled=True)  11.4 us
    unnamed x27, local copies, waits for them, and re-layouts  6.47 us
    all_to_all x1, starting transfers between devices, body(): lax.all_to_all(in_first, 'row', split_axis=2, concat_axis=1, tiled=True)  5.51 us
  transfers between devices with their start and end apart: 3, of which 2 were waited for; matrix products, arithmetic and copies ran while one was open for 1% of the time, Pallas kernels for 0%

commit v1 on v0

--- a/solution.py
+++ b/solution.py
@@ -1,9 +1,257 @@
+import functools
 import jax
 import jax.numpy as jnp
 from jax import lax
+from jax.experimental import pallas as pl
+from jax.experimental.pallas import tpu as pltpu
 from jax.sharding import PartitionSpec as P
 
 epsilon = 1e-05
+MESH = pl.DeviceIdType.MESH
+F32 = jnp.float32
+BF16 = jnp.bfloat16
+
+
+def lane_norm(values, gain, bias):
+    mean_val = jnp.mean(values, axis=-1, keepdims=True)
+    variance = jnp.mean(values * values, axis=-1, keepdims=True) - mean_val * mean_val
+    return ((values - mean_val) * lax.rsqrt(variance + epsilon) * gain + bias).astype(BF16)
+
+
+def dot_nt(a, b):
+    return lax.dot_general(a, b, (((1,), (1,)), ((), ())), preferred_element_type=F32)
+
+
+def dot_nn(a, b):
+    return lax.dot_general(a, b, (((1,), (0,)), ((), ())), preferred_element_type=F32)
+
+
+def window_kernel(
+    rows,
+    chs,
+    mask_ref,
+    chain_ref,
+    small_ref,
+    in_gain_ref,
+    in_bias_ref,
+    weights_ref,
+    out_ref,
+    small_buf,
+    weights_buf,
+    pair_buf,
+    left_buf,
+    right_buf,
+    middle_buf,
+    normed_buf,
+    small_send,
+    small_recv,
+    weights_send,
+    weights_recv,
+    row_send,
+    row_recv,
+    own_sem,
+):
+    n = pair_buf.shape[0]
+    lanes = pair_buf.shape[2]
+    block = lanes // chs
+    row = lax.axis_index("row")
+    ch = lax.axis_index("ch")
+
+    own_copies = [pltpu.make_async_copy(small_ref, small_buf.at[ch], own_sem.at[0])]
+    for u in range(2):
+        own_copies.append(
+            pltpu.make_async_copy(weights_ref.at[u], weights_buf.at[u, ch], own_sem.at[1 + u])
+        )
+    for copy in own_copies:
+        copy.start()
+
+    barrier = pltpu.get_barrier_semaphore()
+    for step in range(1, chs):
+        pl.semaphore_signal(
+            barrier, inc=1, device_id=(row, lax.rem(ch + step, chs)), device_id_type=MESH
+        )
+    for step in range(1, rows):
+        pl.semaphore_signal(
+            barrier, inc=1, device_id=(lax.rem(row + step, rows), ch), device_id_type=MESH
+        )
+    pl.semaphore_wait(barrier, chs - 1 + rows - 1)
+
+    small_copies = []
+    for step in range(1, chs):
+        copy = pltpu.make_async_remote_copy(
+            src_ref=small_ref,
+            dst_ref=small_buf.at[ch],
+            send_sem=small_send.at[step - 1],
+            recv_sem=small_recv.at[step - 1],
+            device_id=(row, lax.rem(ch + step, chs)),
+            device_id_type=MESH,
+        )
+        copy.start()
+        small_copies.append(copy)
+    weight_copies = []
+    for u in range(2):
+        group = []
+        for step in range(1, chs):
+            copy = pltpu.make_async_remote_copy(
+                src_ref=weights_ref.at[u],
+                dst_ref=weights_buf.at[u, ch],
+                send_sem=weights_send.at[u, step - 1],
+                recv_sem=weights_recv.at[u, step - 1],
+                device_id=(row, lax.rem(ch + step, chs)),
+                device_id_type=MESH,
+            )
+            copy.start()
+            group.append(copy)
+        weight_copies.append(group)
+
+    own_copies[0].wait()
+    for copy in small_copies:
+        copy.wait_recv()
+    pair_buf[row] = jnp.concatenate([small_buf[m, :n, :] for m in range(chs)], axis=1)
+
+    row_copies = []
+    for step in range(1, rows):
+        copy = pltpu.make_async_remote_copy(
+            src_ref=pair_buf.at[row],
+            dst_ref=pair_buf.at[row],
+            send_sem=row_send.at[step - 1],
+            recv_sem=row_recv.at[step - 1],
+            device_id=(lax.rem(row + step, rows), ch),
+            device_id_type=MESH,
+        )
+        copy.start()
+        row_copies.append(copy)
+
+    vectors = jnp.concatenate([small_buf[m, n:, :] for m in range(chs)], axis=1)
+    place = lax.broadcasted_iota(jnp.int32, (n, lanes), 0)
+    mask_j = jnp.zeros((n, lanes), jnp.int32)
+    chain_j = jnp.zeros((n, lanes), jnp.int32)
+    for j in range(n):
+        mask_j = jnp.where(place == j, mask_ref[j], mask_j)
+        chain_j = jnp.where(place == j, chain_ref[j], chain_j)
+    pair_mask = jnp.concatenate([(mask_j * mask_ref[i]).astype(F32) for i in range(n)], axis=0)
+    same_chain = jnp.concatenate(
+        [jnp.where(chain_j == chain_ref[i], 1.0, 0.0).astype(F32) for i in range(n)], axis=0
+    )
+    same_here = jnp.where(chain_j == chain_ref[row], 1.0, 0.0).astype(F32)
+
+    def weight(u, part):
+        return weights_buf[u, :, part * block : (part + 1) * block, :].reshape(lanes, lanes)
+
+    def arms(u, normed):
+        left = jax.nn.sigmoid(dot_nt(normed, weight(u, 0))) * dot_nt(normed, weight(u, 1))
+        right = jax.nn.sigmoid(dot_nt(normed, weight(u, 2))) * dot_nt(normed, weight(u, 3))
+        left_buf[...] = (left * pair_mask).astype(BF16).astype(F32)
+        right_buf[...] = (right * pair_mask).astype(BF16).astype(F32)
+
+    def update(u, pair, normed, product, same):
+        xn = lane_norm(product, vectors[2 + u : 3 + u, :], vectors[4 + u : 5 + u, :])
+        mixed = dot_nn(xn, weight(u, 5))
+        gate = jax.nn.sigmoid(dot_nt(normed, weight(u, 4)) + vectors[u : u + 1, :] * same)
+        return (pair + gate * mixed).astype(BF16)
+
+    for copy in row_copies:
+        copy.wait_recv()
+    pair = pair_buf[...].reshape(n * n, lanes)
+    normed = lane_norm(pair, in_gain_ref[0:1, :], in_bias_ref[0:1, :])
+    own_copies[1].wait()
+    for copy in weight_copies[0]:
+        copy.wait_recv()
+    arms(0, normed)
+    right_k = [right_buf[pl.ds(k, n, stride=n), :] for k in range(n)]
+    product = []
+    for i in range(n):
+        total = left_buf[i * n : i * n + 1, :] * right_k[0]
+        for k in range(1, n):
+            total = total + left_buf[i * n + k : i * n + k + 1, :] * right_k[k]
+        product.append(total)
+    middle = update(0, pair, normed, jnp.concatenate(product, axis=0), same_chain).astype(F32)
+    middle_buf[...] = middle
+
+    normed = lane_norm(middle, in_gain_ref[1:2, :], in_bias_ref[1:2, :])
+    normed_buf[...] = normed.astype(F32)
+    own_copies[2].wait()
+    for copy in weight_copies[1]:
+        copy.wait_recv()
+    arms(1, normed)
+    total = left_buf[pl.ds(row, 1), :] * right_buf[0:n, :]
+    for k in range(1, n):
+        total = total + left_buf[pl.ds(k * n + row, 1), :] * right_buf[k * n : (k + 1) * n, :]
+    here = pl.ds(pl.multiple_of(row * n, n), n)
+    result = update(1, middle_buf[here, :], normed_buf[here, :].astype(BF16), total, same_here)
+
+    picked = lax.broadcasted_iota(jnp.int32, (block, lanes), 1)
+    wanted = lax.broadcasted_iota(jnp.int32, (block, lanes), 0) + ch * block
+    chosen = jnp.where(picked == wanted, 1.0, 0.0).astype(BF16)
+    out_ref[...] = dot_nt(chosen, result).astype(BF16)
+
+    for copy in small_copies + weight_copies[0] + weight_copies[1] + row_copies:
+        copy.wait_send()
+
+
+def window_body(
+    rows,
+    chs,
+    pair_rep,
+    residue_mask,
+    chain_ids,
+    in_gain,
+    in_bias,
+    w_proj,
+    w_gate,
+    pair_bias,
+    out_gain,
+    out_bias,
+    w_out,
+):
+    block, _, n = pair_rep.shape
+    lanes = in_gain.shape[1]
+    layers, _, parts, _ = w_proj.shape
+    weights = jnp.concatenate(
+        [
+            jnp.transpose(w_proj, (0, 2, 3, 1)).reshape(layers, parts * block, lanes),
+            jnp.swapaxes(w_gate, 1, 2),
+            w_out,
+        ],
+        axis=1,
+    )
+    small = jnp.concatenate(
+        [
+            jnp.swapaxes(pair_rep[:, 0, :], 0, 1).astype(F32),
+            pair_bias,
+            out_gain,
+            out_bias,
+            jnp.zeros((2, block), F32),
+        ],
+        axis=0,
+    )
+    vmem = pl.BlockSpec(memory_space=pltpu.VMEM)
+    smem = pl.BlockSpec(memory_space=pltpu.SMEM)
+    dma = pltpu.SemaphoreType.DMA
+    out = pl.pallas_call(
+        functools.partial(window_kernel, rows, chs),
+        out_shape=jax.ShapeDtypeStruct((block, n), BF16),
+        in_specs=[smem, smem, vmem, vmem, vmem, vmem],
+        out_specs=vmem,
+        scratch_shapes=[
+            pltpu.VMEM((chs,) + small.shape, F32),
+            pltpu.VMEM((layers, chs) + weights.shape[1:], BF16),
+            pltpu.VMEM((n, n, lanes), F32),
+            pltpu.VMEM((n * n, lanes), F32),
+            pltpu.VMEM((n * n, lanes), F32),
+            pltpu.VMEM((n * n, lanes), F32),
+            pltpu.VMEM((n * n, lanes), F32),
+            dma((chs - 1,)),
+            dma((chs - 1,)),
+            dma((layers, chs - 1)),
+            dma((layers, chs - 1)),
+            dma((rows - 1,)),
+            dma((rows - 1,)),
+            dma((1 + layers,)),
+        ],
+        compiler_params=pltpu.CompilerParams(collective_id=0, has_side_effects=True),
+    )(residue_mask, chain_ids, small, in_gain, in_bias, weights)
+    return out[:, None, :]
 
 
 def channel_norm(values, norm_gain, norm_bias):
@@ -101,9 +349,18 @@
     return (middle.astype(jnp.float32) + update).astype(jnp.bfloat16)
 
 
+def choose(rows, chs, *args):
+    pair_rep, in_gain = args[0], args[3]
+    n, lanes = pair_rep.shape[2], in_gain.shape[1]
+    one_tile = pair_rep.shape[1] == 1 and n == rows == 8 and lanes == 128
+    if one_tile and chs > 1 and args[5].shape[1] == pair_rep.shape[0] * chs:
+        return window_body(rows, chs, *args)
+    return body(*args)
+
+
 def solution(mesh):
     return jax.shard_map(
-        body,
+        functools.partial(choose, mesh.shape["row"], mesh.shape["ch"]),
         mesh=mesh,
         in_specs=(
             P("ch", "row", None),

time: 144 us -> 20.8 us (0.14)
  blocking collectives: 76.7 us -> 0 us
  waiting for transfers between devices: 35.5 us -> 0 us
  Pallas kernels: 0 us -> 14.9 us
  between operations: 13.5 us -> 0.01 us
  starting transfers between devices: 5.55 us -> 0 us
  local copies, waits for them, and re-layouts: 8.5 us -> 3.26 us
  matrix products: 1.71 us -> 0 us
    all_gather x4 -> x0, blocking collectives: 65 us -> none  [the longest x1 27 us: body(): lax.all_gather(second_arm, 'row', axis=1, tiled=True)]
    unnamed x4 -> x0, waiting for transfers between devices: 35.5 us -> none
    pallas_call x0 -> x1, Pallas kernels: none -> 14.9 us  [window_body(): pl.pallas_call(functools.partial(window_kernel, rows, chs), out_shape=jax...]
    psum x2 -> x0, blocking collectives: 11.6 us -> none  [finish(): lax.psum((jnp.sum(product_sum, axis=0), jnp.sum(product_sum * product_sum...]
    unnamed x27 -> x2, local copies, waits for them, and re-layouts: 6.47 us -> 0.01 us
    all_to_all x1 -> x0, starting transfers between devices: 5.51 us -> none  [body(): lax.all_to_all(in_first, 'row', split_axis=2, concat_axis=1, tiled=True)]
    concatenate x0 -> x1, local copies, waits for them, and re-layouts: none -> 1.91 us  [window_body(): jnp.concatenate([jnp.swapaxes(pair_rep[:, 0, :], 0, 1).astype(F32), pair_...]
    dot_general x6 -> x0, matrix products: 1.71 us -> none  [the longest x2 0.98 us: prepare(): jnp.einsum('cij,cd->dij', normed, w_gate[layer], preferred_element_type=j...]
  transfers between devices with their start and end apart: 3 -> 0, of which waited for: 2 -> 0; matrix products, arithmetic and copies ran while one was open for 1% -> 0% of each run, Pallas kernels for 0% -> 0%
where the time goes in v1:
time: 20.8 us; the launch traced here: 20.4 us
  Pallas kernels  14.9 us (72%)
  local copies, waits for them, and re-layouts  3.26 us (16%)
  other arithmetic  2.2 us (11%)
    pallas_call x1, Pallas kernels, window_body(): pl.pallas_call(functools.partial(window_kernel, rows, chs), out_shape=jax...  14.9 us
    concatenate x1, local copies, waits for them, and re-layouts, window_body(): jnp.concatenate([jnp.swapaxes(pair_rep[:, 0, :], 0, 1).astype(F32), pair_...  1.91 us
    concatenate x1, other arithmetic, window_body(): jnp.concatenate([jnp.transpose(w_proj, (0, 2, 3, 1)).reshape(layers, part...  1.5 us
    broadcast_in_dim x1, local copies, waits for them, and re-layouts, window_body(): return out[:, None, :]  1.35 us
    convert_element_type x1, other arithmetic, window_body(): jnp.swapaxes(pair_rep[:, 0, :], 0, 1).astype(F32)  0.7 us

profile of v1, /device:TPU:0, one launch (start us, length us, event | category | flops | bytes accessed | tf_op | source)
XLA Modules:
  0.0 20.4 jit_solution(16405054800007038118)
XLA Ops:
  0.0 0.0 copy-start
  0.0 0.7 %convert_bitcast_fusion = f32[8,32]{1,0:T(8,128)S(1)} fusion(bf16[32,1,8]{0,2,1:T(8,128)(2,1)} %param.11), kind=kLoop, calls=%fused_computation.1 | loop fusion | flops 256 | bytes 1536 | tf_op jit(solution)/shard_map/convert_element_type | solution.py:220
  0.7 1.9 %concatenate.6.small_ref = f32[16,32]{1,0:T(8,128)} concatenate(f32[8,32]{1,0:T(8,128)S(1)} %convert_bitcast_fusion, f32[2,32]{1,0:T(2,128)} %param.18, f32[2,32]{1,0:T(2,128)} %param.19, f32[2,32]{1,0:T(2,128)} %param.20, f32[2,32]{1,0:T(2,128)S(1)} %broadcast_in_dim.6), dimensions={0} | concatenate | bytes 4096 | tf_op jit(solution)/shard_map/concatenate | solution.py:218
  2.6 0.0 copy-done
  2.6 1.5 %pad_maximum_fusion.weights_ref = bf16[2,192,128]{2,1,0:T(8,128)(2,1)} fusion(bf16[2,32,128]{2,1,0:T(8,128)(2,1)S(1)} %copy-done, bf16[2,32,128]{2,1,0:T(8,128)(2,1)} %bitcast.12, bf16[2,128,128]{2,1,0:T(8,128)(2,1)} %bitcast.10), kind=kLoop, calls=%fused_computation | loop fusion | flops 294912 | bytes 196608 | tf_op jit(solution)/shard_map/concatenate | solution.py:210
  4.1 14.9 %shard_map.109 = bf16[32,8]{1,0:T(8,128)(2,1)} custom-call(s32[8]{0:T(128)} %mask_ref.1, s32[8]{0:T(128)} %chain_ref.1, f32[16,32]{1,0:T(8,128)} %concatenate.6.small_ref, f32[2,128]{1,0:T(2,128)} %in_gain_ref.1, f32[2,128]{1,0:T(2,128)} %in_bias_ref.1, bf16[2,192,128]{2,1,0:T(8,128)(2,1)} %pad_maximum_fusion.weights_ref), custom_call_target="tpu_custom_call" | custom-call | tf_op jit(solution)/shard_map/pallas_call | solution.py:231
  19.1 1.3 %copy.12 = bf16[32,1,8]{0,2,1:T(8,128)(2,1)} copy(bf16[32,1,8]{2,0,1:T(8,128)(2,1)} %bitcast.11) | data formatting | bytes 1024 | tf_op jit(solution)/shard_map/broadcast_in_dim | solution.py:254
  (1 shorter events, 0.0 us)
Async XLA Ops:
  0.0 2.6 %copy-start = (bf16[2,32,128]{2,1,0:T(8,128)(2,1)S(1)}, bf16[2,32,128]{2,1,0:T(8,128)(2,1)}, u32[]{:S(2)}) copy-start(bf16[2,32,128]{2,1,0:T(8,128)(2,1)} %param.21) | copy-start | bytes 49156

commit v2 on v1

--- a/solution.py
+++ b/solution.py
@@ -31,22 +31,32 @@
     chs,
     mask_ref,
     chain_ref,
-    small_ref,
+    pair_ref,
     in_gain_ref,
     in_bias_ref,
-    weights_ref,
+    proj_ref,
+    gate_ref,
+    bias_ref,
+    gain_ref,
+    offset_ref,
+    mix_ref,
     out_ref,
-    small_buf,
-    weights_buf,
+    block_buf,
+    proj_buf,
+    gate_buf,
+    mix_buf,
+    vector_buf,
     pair_buf,
     left_buf,
     right_buf,
     middle_buf,
     normed_buf,
-    small_send,
-    small_recv,
-    weights_send,
-    weights_recv,
+    block_send,
+    block_recv,
+    vector_send,
+    vector_recv,
+    weight_send,
+    weight_recv,
     row_send,
     row_recv,
     own_sem,
@@ -57,14 +67,6 @@
     row = lax.axis_index("row")
     ch = lax.axis_index("ch")
 
-    own_copies = [pltpu.make_async_copy(small_ref, small_buf.at[ch], own_sem.at[0])]
-    for u in range(2):
-        own_copies.append(
-            pltpu.make_async_copy(weights_ref.at[u], weights_buf.at[u, ch], own_sem.at[1 + u])
-        )
-    for copy in own_copies:
-        copy.start()
-
     barrier = pltpu.get_barrier_semaphore()
     for step in range(1, chs):
         pl.semaphore_signal(
@@ -74,41 +76,78 @@
         pl.semaphore_signal(
             barrier, inc=1, device_id=(lax.rem(row + step, rows), ch), device_id_type=MESH
         )
-    pl.semaphore_wait(barrier, chs - 1 + rows - 1)
-
-    small_copies = []
-    for step in range(1, chs):
-        copy = pltpu.make_async_remote_copy(
-            src_ref=small_ref,
-            dst_ref=small_buf.at[ch],
-            send_sem=small_send.at[step - 1],
-            recv_sem=small_recv.at[step - 1],
-            device_id=(row, lax.rem(ch + step, chs)),
-            device_id_type=MESH,
-        )
-        copy.start()
-        small_copies.append(copy)
-    weight_copies = []
+
+    first = [(pair_ref, block_buf.at[ch], 0, block_send, block_recv)]
+    vectors_out = [
+        (ref, vector_buf.at[t, ch], 1 + t, vector_send.at[t], vector_recv.at[t])
+        for t, ref in enumerate((bias_ref, gain_ref, offset_ref))
+    ]
+    weights_out = []
     for u in range(2):
         group = []
-        for step in range(1, chs):
-            copy = pltpu.make_async_remote_copy(
-                src_ref=weights_ref.at[u],
-                dst_ref=weights_buf.at[u, ch],
-                send_sem=weights_send.at[u, step - 1],
-                recv_sem=weights_recv.at[u, step - 1],
-                device_id=(row, lax.rem(ch + step, chs)),
-                device_id_type=MESH,
+        for t, (ref, buf) in enumerate(
+            ((proj_ref, proj_buf), (gate_ref, gate_buf), (mix_ref, mix_buf))
+        ):
+            group.append(
+                (
+                    ref.at[u],
+                    buf.at[u, ch],
+                    4 + 3 * u + t,
+                    weight_send.at[u, t],
+                    weight_recv.at[u, t],
+                )
             )
+        weights_out.append(group)
+
+    def keep(items):
+        copies = [pltpu.make_async_copy(src, dst, own_sem.at[k]) for src, dst, k, _, _ in items]
+        for copy in copies:
             copy.start()
-            group.append(copy)
-        weight_copies.append(group)
-
-    own_copies[0].wait()
-    for copy in small_copies:
-        copy.wait_recv()
-    pair_buf[row] = jnp.concatenate([small_buf[m, :n, :] for m in range(chs)], axis=1)
-
+        return copies
+
+    def spread(items):
+        copies = []
+        for src, dst, _, send, recv in items:
+            for step in range(1, chs):
+                copy = pltpu.make_async_remote_copy(
+                    src_ref=src,
+                    dst_ref=dst,
+                    send_sem=send.at[step - 1],
+                    recv_sem=recv.at[step - 1],
+                    device_id=(row, lax.rem(ch + step, chs)),
+                    device_id_type=MESH,
+                )
+                copy.start()
+                copies.append(copy)
+        return copies
+
+    def arrive(own, remote):
+        for copy in own:
+            copy.wait()
+        for copy in remote:
+            copy.wait_recv()
+
+    own_first = keep(first)
+    own_weights = [keep(weights_out[0] + vectors_out), keep(weights_out[1])]
+
+    place = lax.broadcasted_iota(jnp.int32, (n, lanes), 0)
+    mask_j = jnp.zeros((n, lanes), jnp.int32)
+    chain_j = jnp.zeros((n, lanes), jnp.int32)
+    for j in range(n):
+        mask_j = jnp.where(place == j, mask_ref[j], mask_j)
+        chain_j = jnp.where(place == j, chain_ref[j], chain_j)
+    pair_mask = jnp.concatenate([(mask_j * mask_ref[i]).astype(F32) for i in range(n)], axis=0)
+    same_chain = jnp.concatenate(
+        [jnp.where(chain_j == chain_ref[i], 1.0, 0.0).astype(F32) for i in range(n)], axis=0
+    )
+    same_here = jnp.where(chain_j == chain_ref[row], 1.0, 0.0).astype(F32)
+
+    pl.semaphore_wait(barrier, chs - 1 + rows - 1)
+    remote_first = spread(first)
+    remote_weights = [spread(weights_out[0] + vectors_out), spread(weights_out[1])]
+
+    arrive(own_first, remote_first)
+    pair_buf[row] = jnp.concatenate([block_buf[m].astype(F32) for m in range(chs)], axis=1)
     row_copies = []
     for step in range(1, rows):
         copy = pltpu.make_async_remote_copy(
@@ -122,41 +161,29 @@
         copy.start()
         row_copies.append(copy)
 
-    vectors = jnp.concatenate([small_buf[m, n:, :] for m in range(chs)], axis=1)
-    place = lax.broadcasted_iota(jnp.int32, (n, lanes), 0)
-    mask_j = jnp.zeros((n, lanes), jnp.int32)
-    chain_j = jnp.zeros((n, lanes), jnp.int32)
-    for j in range(n):
-        mask_j = jnp.where(place == j, mask_ref[j], mask_j)
-        chain_j = jnp.where(place == j, chain_ref[j], chain_j)
-    pair_mask = jnp.concatenate([(mask_j * mask_ref[i]).astype(F32) for i in range(n)], axis=0)
-    same_chain = jnp.concatenate(
-        [jnp.where(chain_j == chain_ref[i], 1.0, 0.0).astype(F32) for i in range(n)], axis=0
-    )
-    same_here = jnp.where(chain_j == chain_ref[row], 1.0, 0.0).astype(F32)
-
-    def weight(u, part):
-        return weights_buf[u, :, part * block : (part + 1) * block, :].reshape(lanes, lanes)
+    def projection(u, part):
+        here = slice(part * block, (part + 1) * block)
+        return proj_buf[u, :, here, :].reshape(lanes, lanes)
+
+    def vector(t, u):
+        return jnp.concatenate([vector_buf[t, m, u : u + 1, :] for m in range(chs)], axis=1)
 
     def arms(u, normed):
-        left = jax.nn.sigmoid(dot_nt(normed, weight(u, 0))) * dot_nt(normed, weight(u, 1))
-        right = jax.nn.sigmoid(dot_nt(normed, weight(u, 2))) * dot_nt(normed, weight(u, 3))
+        left = jax.nn.sigmoid(dot_nt(normed, projection(u, 0))) * dot_nt(normed, projection(u, 1))
+        right = jax.nn.sigmoid(dot_nt(normed, projection(u, 2))) * dot_nt(normed, projection(u, 3))
         left_buf[...] = (left * pair_mask).astype(BF16).astype(F32)
         right_buf[...] = (right * pair_mask).astype(BF16).astype(F32)
 
     def update(u, pair, normed, product, same):
-        xn = lane_norm(product, vectors[2 + u : 3 + u, :], vectors[4 + u : 5 + u, :])
-        mixed = dot_nn(xn, weight(u, 5))
-        gate = jax.nn.sigmoid(dot_nt(normed, weight(u, 4)) + vectors[u : u + 1, :] * same)
-        return (pair + gate * mixed).astype(BF16)
-
-    for copy in row_copies:
-        copy.wait_recv()
+        xn = lane_norm(product, vector(1, u), vector(2, u))
+        mixed = dot_nn(xn, mix_buf[u].reshape(lanes, lanes))
+        logits = dot_nt(normed, gate_buf[u].reshape(lanes, lanes)) + vector(0, u) * same
+        return (pair + jax.nn.sigmoid(logits) * mixed).astype(BF16)
+
+    arrive([], row_copies)
     pair = pair_buf[...].reshape(n * n, lanes)
     normed = lane_norm(pair, in_gain_ref[0:1, :], in_bias_ref[0:1, :])
-    own_copies[1].wait()
-    for copy in weight_copies[0]:
-        copy.wait_recv()
+    arrive(own_weights[0], remote_weights[0])
     arms(0, normed)
     right_k = [right_buf[pl.ds(k, n, stride=n), :] for k in range(n)]
     product = []
@@ -170,9 +197,7 @@
 
     normed = lane_norm(middle, in_gain_ref[1:2, :], in_bias_ref[1:2, :])
     normed_buf[...] = normed.astype(F32)
-    own_copies[2].wait()
-    for copy in weight_copies[1]:
-        copy.wait_recv()
+    arrive(own_weights[1], remote_weights[1])
     arms(1, normed)
     total = left_buf[pl.ds(row, 1), :] * right_buf[0:n, :]
     for k in range(1, n):
@@ -183,9 +208,9 @@
     picked = lax.broadcasted_iota(jnp.int32, (block, lanes), 1)
     wanted = lax.broadcasted_iota(jnp.int32, (block, lanes), 0) + ch * block
     chosen = jnp.where(picked == wanted, 1.0, 0.0).astype(BF16)
-    out_ref[...] = dot_nt(chosen, result).astype(BF16)
-
-    for copy in small_copies + weight_copies[0] + weight_copies[1] + row_copies:
+    out_ref[...] = dot_nt(result, chosen).astype(BF16)
+
+    for copy in remote_first + remote_weights[0] + remote_weights[1] + row_copies:
         copy.wait_send()
 
 
@@ -207,35 +232,20 @@
     block, _, n = pair_rep.shape
     lanes = in_gain.shape[1]
     layers, _, parts, _ = w_proj.shape
-    weights = jnp.concatenate(
-        [
-            jnp.transpose(w_proj, (0, 2, 3, 1)).reshape(layers, parts * block, lanes),
-            jnp.swapaxes(w_gate, 1, 2),
-            w_out,
-        ],
-        axis=1,
-    )
-    small = jnp.concatenate(
-        [
-            jnp.swapaxes(pair_rep[:, 0, :], 0, 1).astype(F32),
-            pair_bias,
-            out_gain,
-            out_bias,
-            jnp.zeros((2, block), F32),
-        ],
-        axis=0,
-    )
     vmem = pl.BlockSpec(memory_space=pltpu.VMEM)
     smem = pl.BlockSpec(memory_space=pltpu.SMEM)
     dma = pltpu.SemaphoreType.DMA
     out = pl.pallas_call(
         functools.partial(window_kernel, rows, chs),
-        out_shape=jax.ShapeDtypeStruct((block, n), BF16),
-        in_specs=[smem, smem, vmem, vmem, vmem, vmem],
+        out_shape=jax.ShapeDtypeStruct((n, block), BF16),
+        in_specs=[smem, smem] + [vmem] * 9,
         out_specs=vmem,
         scratch_shapes=[
-            pltpu.VMEM((chs,) + small.shape, F32),
-            pltpu.VMEM((layers, chs) + weights.shape[1:], BF16),
+            pltpu.VMEM((chs, n, block), BF16),
+            pltpu.VMEM((layers, chs, parts * block, lanes), BF16),
+            pltpu.VMEM((layers, chs, block, lanes), BF16),
+            pltpu.VMEM((layers, chs, block, lanes), BF16),
+            pltpu.VMEM((3, chs, layers, block), F32),
             pltpu.VMEM((n, n, lanes), F32),
             pltpu.VMEM((n * n, lanes), F32),
             pltpu.VMEM((n * n, lanes), F32),
@@ -243,15 +253,29 @@
             pltpu.VMEM((n * n, lanes), F32),
             dma((chs - 1,)),
             dma((chs - 1,)),
-            dma((layers, chs - 1)),
-            dma((layers, chs - 1)),
+            dma((3, chs - 1)),
+            dma((3, chs - 1)),
+            dma((layers, 3, chs - 1)),
+            dma((layers, 3, chs - 1)),
             dma((rows - 1,)),
             dma((rows - 1,)),
-            dma((1 + layers,)),
+            dma((4 + 3 * layers,)),
         ],
         compiler_params=pltpu.CompilerParams(collective_id=0, has_side_effects=True),
-    )(residue_mask, chain_ids, small, in_gain, in_bias, weights)
-    return out[:, None, :]
+    )(
+        residue_mask,
+        chain_ids,
+        jnp.swapaxes(pair_rep[:, 0, :], 0, 1),
+        in_gain,
+        in_bias,
+        jnp.transpose(w_proj, (0, 2, 3, 1)).reshape(layers, parts * block, lanes),
+        jnp.swapaxes(w_gate, 1, 2),
+        pair_bias,
+        out_gain,
+        out_bias,
+        w_out,
+    )
+    return jnp.swapaxes(out, 0, 1)[:, None, :]
 
 
 def channel_norm(values, norm_gain, norm_bias):

time: 20.8 us -> 16.7 us (0.80)
  other arithmetic: 2.2 us -> 0 us
  local copies, waits for them, and re-layouts: 3.26 us -> 1.26 us
  Pallas kernels: 14.9 us -> 15.2 us
    concatenate x1 -> x0, local copies, waits for them, and re-layouts: 1.91 us -> none  [window_body(): jnp.concatenate([jnp.swapaxes(pair_rep[:, 0, :], 0, 1).astype(F32), pair_...]
    concatenate x1 -> x0, other arithmetic: 1.5 us -> none  [window_body(): jnp.concatenate([jnp.transpose(w_proj, (0, 2, 3, 1)).reshape(layers, part...]
    broadcast_in_dim x2 -> x0, local copies, waits for them, and re-layouts: 1.35 us -> none  [the longest x1 1.35 us: window_body(): return out[:, None, :]]
    unnamed x2 -> x1, local copies, waits for them, and re-layouts: 0.01 us -> 1.26 us
    convert_element_type x1 -> x0, other arithmetic: 0.7 us -> none  [window_body(): jnp.swapaxes(pair_rep[:, 0, :], 0, 1).astype(F32)]
    pallas_call x1, Pallas kernels: 14.9 us -> 15.2 us  [window_body(): pl.pallas_call(functools.partial(window_kernel, rows, chs), out_shape=jax...]
where the time goes in v2:
time: 16.7 us; the launch traced here: 16.5 us
  Pallas kernels  15.2 us (91%)
  local copies, waits for them, and re-layouts  1.26 us (8%)
    pallas_call x1, Pallas kernels, window_body(): pl.pallas_call(functools.partial(window_kernel, rows, chs), out_shape=jax...  15.2 us
    unnamed x1, local copies, waits for them, and re-layouts  1.26 us

profile of v2, /device:TPU:0, one launch (start us, length us, event | category | flops | bytes accessed | tf_op | source)
XLA Modules:
  0.0 16.5 jit_solution(8755897363414991142)
XLA Ops:
  0.0 15.2 %shard_map.109 = bf16[8,32]{1,0:T(8,128)(2,1)} custom-call(s32[8]{0:T(128)} %mask_ref.1, s32[8]{0:T(128)} %chain_ref.1, bf16[8,32]{1,0:T(8,128)(2,1)} %bitcast.13, f32[2,128]{1,0:T(2,128)} %in_gain_ref.1, f32[2,128]{1,0:T(2,128)} %in_bias_ref.1, bf16[2,128,128]{2,1,0:T(8,128)(2,1)} %bitcast.10, bf16[2,32,128]{2,1,0:T(8,128)(2,1)} %bitcast.11, ...), custom_call_target="tpu_custom_call" | custom-call | tf_op jit(solution)/shard_map/pallas_call | solution.py:238
  15.2 1.3 %copy.13 = bf16[32,1,8]{0,2,1:T(8,128)(2,1)} copy(bf16[32,1,8]{0,2,1:T(8,128)(2,1)} %bitcast.12) | data formatting | bytes 1024
